TPU v7x, 32 devices: a whole 2x2x4 slice. The times are simulated.
32 devices in a mesh: dp: 8 (over y, x, core), fsdp: 4 (over z).
Axes of the slice: x: 2, y: 2, z: 4, core: 2. Of those that a mesh axis runs over, the one named last changes fastest.
Arguments:
- gradients: bfloat16 [8, 512, 8192], P('dp', None, 'fsdp'), may hold values from -1.5 to 1.5
- momentum: float32 [512, 8192], P('dp', 'fsdp'), may hold values from -1500 to 1500
- weight: float32 [512, 8192], P(None, 'fsdp'), may hold values from -3 to 3
- logit_peaks: int32 [32, 32], P(('dp', 'fsdp')), may hold values from 0 to 479, as said below
- clip_threshold: int32 [1], replicated, may hold values from 60 to 120
Outputs:
- new_weight: float32 [512, 8192], P(None, 'fsdp')
- new_momentum: float32 [512, 8192], P('dp', 'fsdp')
- update_norm: float32 [1], replicated
Inputs may be any that keep to these rules, and one draw needn't show every extreme that they name: `logit_peaks`: for every head, the largest entry over all rows is at least 40.
All inputs are finite; a program needn't handle non-finite values.
Results may differ from a plain program's by a relative error of at most 0.0023.
Values may be sent and summed in bfloat16 or wider, within the bound.
A program may use at most 64 MiB of HBM per device.

v0:
```python
import math
import jax
import jax.numpy as jnp
from jax import lax
from jax.sharding import PartitionSpec as P

KVL = 512
NOPE = 128
VDIM = 128
HEADS = 32
ITERS = 3
KVO = 8192
quintic_terms = (3.4445, -4.775, 2.0315)
learning_rate = 0.5
weight_decay = 0.1
momentum_decay = 0.95
update_gain = 0.2
epsilon = 1e-07


def column_factors(global_peaks, clip_threshold):
    largest = jnp.max(global_peaks, axis=0).astype(jnp.float32)
    clip_ratio = jnp.minimum(1.0, clip_threshold.astype(jnp.float32)[0] / largest)
    key_scale = jnp.sqrt(clip_ratio)
    per_head = jnp.concatenate(
        [jnp.broadcast_to(key_scale[:, None], (HEADS, NOPE)), jnp.ones((HEADS, VDIM), jnp.float32)],
        axis=1,
    )
    return per_head.reshape(HEADS * (NOPE + VDIM))


def gram_over_replicas(partial_gram):
    return lax.psum(partial_gram.astype(jnp.bfloat16), "dp").astype(jnp.float32)


def newton_schulz(column_block, gram_sum):
    current = column_block
    for iteration in range(ITERS):
        partial_gram = lax.dot_general(
            current,
            current,
            (((1,), (1,)), ((), ())),
            precision=lax.Precision.HIGHEST,
            preferred_element_type=jnp.float32,
        )
        square = gram_sum(partial_gram)
        combined = quintic_terms[1] * square + quintic_terms[2] * jnp.dot(
            square, square, precision=lax.Precision.HIGHEST, preferred_element_type=jnp.float32
        )
        current = quintic_terms[0] * current + jnp.dot(
            combined, current, precision=lax.Precision.HIGHEST, preferred_element_type=jnp.float32
        )
    return current


def local(gradients, momentum, weight, logit_peaks, clip_threshold):
    replica_shard = gradients[0].astype(jnp.float32)
    summed = lax.psum_scatter(
        replica_shard.astype(jnp.bfloat16), "dp", scatter_dimension=0, tiled=True
    ).astype(jnp.float32)
    new_momentum = momentum_decay * momentum + summed
    blended = summed + momentum_decay * new_momentum
    global_peaks = lax.pmax(logit_peaks, ("dp", "fsdp"))
    square_total = lax.psum(jnp.sum(blended * blended), ("dp", "fsdp"))
    update_norm = jnp.sqrt(square_total / (KVL * KVO)).reshape(1)
    normalized = blended / (jnp.sqrt(square_total) + epsilon)
    dp_count = lax.axis_size("dp")
    fsdp_count = lax.axis_size("fsdp")
    row_count = normalized.shape[0]
    shard_cols = normalized.shape[1]
    piece_cols = shard_cols // dp_count
    wide_rows = lax.all_gather(normalized.astype(jnp.bfloat16), "fsdp", axis=1, tiled=True).astype(
        normalized.dtype
    )
    split_up = wide_rows.reshape(row_count, fsdp_count, dp_count, piece_cols)
    columns = lax.all_to_all(
        split_up.astype(jnp.bfloat16), "dp", split_axis=2, concat_axis=0, tiled=True
    ).astype(split_up.dtype)
    column_block = columns.reshape(KVL, fsdp_count * piece_cols)
    orthogonal = newton_schulz(column_block, gram_over_replicas)
    orthogonal_all = orthogonal.reshape(KVL, fsdp_count, piece_cols)
    own_block = lax.dynamic_index_in_dim(orthogonal_all, lax.axis_index("fsdp"), 1, keepdims=False)
    shard_orthogonal = lax.all_gather(
        own_block.astype(jnp.bfloat16), "dp", axis=1, tiled=True
    ).astype(own_block.dtype)
    update_scale = update_gain * math.sqrt(max(KVL, KVO))
    stepped = weight - learning_rate * (update_scale * shard_orthogonal + weight_decay * weight)
    factors = column_factors(global_peaks, clip_threshold)
    shard_factors = lax.dynamic_slice_in_dim(
        factors, lax.axis_index("fsdp") * shard_cols, shard_cols
    )
    new_weight = stepped * shard_factors[None, :]
    return (new_weight, new_momentum, update_norm)


def solution(mesh):
    placed = (P("dp", None, "fsdp"), P("dp", "fsdp"), P(None, "fsdp"), P(("dp", "fsdp"), None), P())
    return jax.shard_map(
        local,
        mesh=mesh,
        in_specs=placed,
        out_specs=(P(None, "fsdp"), P("dp", "fsdp"), P()),
        check_vma=False,
    )
```

profile of v0, /device:TPU:0, one launch (start us, length us, event | category | flops | bytes accessed | tf_op | source)
XLA Modules:
  0.0 393.2 jit_solution(4246581110344312407)
XLA Ops:
  7.2 0.7 reduce-scatter.2.cloned.1.call-update
  8.0 47.2 %reduce-scatter.2.cloned.1.call-done = bf16[64,2048]{1,0:T(8,128)(2,1)} async-done(((bf16[512,2048]{1,0:T(8,128)(2,1)}), bf16[64,2048]{1,0:T(8,128)(2,1)}) %reduce-scatter.2.cloned.1.call-update) | async-done | bytes 262160 | tf_op jit(solution)/shard_map/reduce_scatter | solution.py:58
  55.1 1.7 multiply_reduce_fusion
  56.8 39.5 %psum.28 = f32[]{:T(128)} all-reduce(f32[]{:T(128)} %get-tuple-element.3), channel_id=1, replica_groups=mesh['dp'=8,'fsdp'=4] {'dp','fsdp'}, use_global_device_ids=true, to_apply=%region_2.0 | all-reduce | flops 1 | bytes 8 | tf_op jit(solution)/shard_map/psum | solution.py:64
  97.0 1.7 divide_convert_fusion
  98.7 0.0 all-reduce.5.cloned.1.call-start
  98.8 29.1 %all-gather.4.cloned.1.call-done = bf16[64,8192]{1,0:T(8,128)(2,1)} async-done(((bf16[64,2048]{1,0:T(8,128)(2,1)}), bf16[64,8192]{1,0:T(8,128)(2,1)}) %all-gather.4.cloned.1.call-update) | async-done | bytes 1048592 | tf_op jit(solution)/shard_map/all_gather | solution.py:72
  127.9 1.5 copy.11
  129.3 0.4 copy.8
  129.8 18.8 %all_to_all.18 = bf16[64,4,8,256]{3,1,0,2:T(4,128)(2,1)S(1)} all-to-all(bf16[64,4,8,256]{3,1,0,2:T(4,128)(2,1)S(1)} %copy.8), channel_id=1, replica_groups=mesh['dp'=8,'fsdp'=4] {'dp'}, dimensions={2} | all-to-all | bytes 2097152 | tf_op jit(solution)/shard_map/all_to_all | solution.py:76
  148.6 0.2 copy.12
  148.8 1.5 convolution_convert_fusion.2
  150.4 52.5 %all-reduce.5.cloned.1.call-done = bf16[512,512]{1,0:T(8,128)(2,1)} async-done(((bf16[512,512]{1,0:T(8,128)(2,1)}), bf16[512,512]{1,0:T(8,128)(2,1)}) %all-reduce.5.cloned.1.call-update) | async-done | bytes 524304 | tf_op jit(solution)/shard_map/psum | solution.py:33
  202.9 1.9 fusion.5
  204.8 1.8 multiply_add_fusion.2
  206.6 1.3 copy-done
  207.9 4.3 %convolution_convert_fusion.1 = bf16[512,512]{1,0:T(8,128)(2,1)} fusion(f32[512,1024]{1,0:T(8,128)S(1)} %multiply_add_fusion.2), kind=kOutput, calls=%fused_computation.14 | convolution fusion | flops 3221487616 | bytes 2621440 | tf_op jit(solution)/shard_map/dot_general | solution.py:39
  212.3 0.2 all-reduce.9.cloned.1.call-start
  212.5 54.0 %all-reduce.7.cloned.1.call-done = bf16[512,512]{1,0:T(8,128)(2,1)} async-done(((bf16[512,512]{1,0:T(8,128)(2,1)}), bf16[512,512]{1,0:T(8,128)(2,1)}) %all-reduce.7.cloned.1.call-update) | async-done | bytes 524304 | tf_op jit(solution)/shard_map/psum | solution.py:33
  266.5 1.9 fusion.4
  268.5 0.1 copy-done.1
  268.6 3.7 multiply_add_fusion.1
  272.2 4.3 %convolution_convert_fusion = bf16[512,512]{1,0:T(8,128)(2,1)} fusion(f32[512,1024]{1,0:T(8,128)S(1)} %multiply_add_fusion.1), kind=kOutput, calls=%fused_computation.13 | convolution fusion | flops 3221487616 | bytes 2621440 | tf_op jit(solution)/shard_map/dot_general | solution.py:39
  276.6 54.2 %all-reduce.9.cloned.1.call-done = bf16[512,512]{1,0:T(8,128)(2,1)} async-done(((bf16[512,512]{1,0:T(8,128)(2,1)}), bf16[512,512]{1,0:T(8,128)(2,1)}) %all-reduce.9.cloned.1.call-update) | async-done | bytes 524304 | tf_op jit(solution)/shard_map/psum | solution.py:33
  330.9 1.9 fusion.3
  332.8 3.6 multiply_add_fusion
  336.4 0.8 reshape.40
  337.2 0.5 constant_dynamic-slice_fusion
  337.7 0.7 copy.15
  338.5 39.3 %pmax.7 = s32[1,32]{1,0:T(1,128)S(1)} all-reduce(s32[1,32]{1,0:T(1,128)S(1)} %copy-done.4), channel_id=1, replica_groups=mesh['dp'=8,'fsdp'=4] {'dp','fsdp'}, use_global_device_ids=true, to_apply=%region_6.0 | all-reduce | flops 32 | bytes 256 | tf_op jit(solution)/shard_map/pmax | solution.py:63
  378.4 0.1 broadcast_in_dim.2
  379.3 5.9 %fusion.2 = f32[512,2048]{1,0:T(8,128)} fusion(f32[512,2048]{1,0:T(8,128)} %param.7, bf16[512,1,2048]{2,0,1:T(8,128)(2,1)} %all-gather.6.cloned.1.call-done, f32[2048]{0:T(1024)S(1)} %dynamic_slice.8), kind=kLoop, calls=%fused_computation.3 | loop fusion | flops 7340032 | bytes 10493952 | tf_op jit(solution)/shard_map/mul | solution.py:92
  (22 shorter events, 0.3 us)
Async XLA Ops:
  7.2 48.0 %copy-start.3 = (f32[64,2048]{1,0:T(8,128)S(1)}, f32[64,2048]{1,0:T(8,128)}, u32[]{:S(2)}) copy-start(f32[64,2048]{1,0:T(8,128)} %param.6) | copy-start | bytes 1572868
  7.2 48.0 %reduce-scatter.2.cloned.1.call-start = ((), (), s32[]{:S(2)}) async-start(), calls=%async_computation.2 | async-start | bytes 2359296 | tf_op jit(solution)/shard_map/reduce_scatter | solution.py:58
  7.9 120.0 %all-gather.4.cloned.1.call-start = ((), (), s32[]{:S(2)}) async-start(), calls=%async_computation.3 | async-start | bytes 1310720 | tf_op jit(solution)/shard_map/all_gather | solution.py:72
  56.8 72.9 %copy-start.2 = (f32[64,2048]{1,0:T(8,128)}, f32[64,2048]{1,0:T(8,128)S(1)}, u32[]{:S(2)}) copy-start(f32[64,2048]{1,0:T(8,128)S(1)} %get-tuple-element.4) | copy-start | bytes 1572868
  98.7 104.1 %all-reduce.5.cloned.1.call-start = ((), (), s32[]{:S(2)}) async-start(), calls=%async_computation.4 | async-start | bytes 1048576 | tf_op jit(solution)/shard_map/psum | solution.py:33
  150.3 116.2 %all-reduce.7.cloned.1.call-start = ((), (), s32[]{:S(2)}) async-start(), calls=%async_computation.5 | async-start | bytes 1048576 | tf_op jit(solution)/shard_map/psum | solution.py:33
  206.6 1.3 copy-start
  212.3 118.6 %all-reduce.9.cloned.1.call-start = ((), (), s32[]{:S(2)}) async-start(), calls=%async_computation.6 | async-start | bytes 1048576 | tf_op jit(solution)/shard_map/psum | solution.py:33
  266.5 2.1 copy-start.1
  276.6 102.7 %all-gather.6.cloned.1.call-start = ((), (), s32[]{:S(2)}) async-start(), calls=%async_computation.7 | async-start | bytes 2359296 | tf_op jit(solution)/shard_map/all_gather | solution.py:83
  336.4 2.1 copy-start.4
Sparse Core Ops, SparseCore 0:
  11.3 43.8 reduce-scatter.1
  98.9 28.9 all-gather.3
  150.5 52.3 all-reduce.4
  212.4 54.0 all-reduce.6
  276.7 54.1 all-reduce.8
  338.6 27.4 all-gather.5
where the time goes:
time: 394 us; the launch traced here: 393 us
  waiting for transfers between devices  238 us (60%)
  blocking collectives  97.5 us (25%)
  matrix products  25 us (6%)
  between operations  17.4 us (4%)
  other arithmetic  9.38 us (2%)
  local copies, waits for them, and re-layouts  5.74 us (1%)
    psum x3, waiting for transfers between devices, gram_over_replicas(): return lax.psum(partial_gram.astype(jnp.bfloat16), 'dp').astype(jnp.float32)  161 us
    reduce_scatter x1, waiting for transfers between devices, local(): lax.psum_scatter(replica_shard.astype(jnp.bfloat16), 'dp', scatter_dimens...  47.2 us
    psum x1, blocking collectives, local(): square_total = lax.psum(jnp.sum(blended * blended), ('dp', 'fsdp'))  39.5 us
    pmax x1, blocking collectives, local(): global_peaks = lax.pmax(logit_peaks, ('dp', 'fsdp'))  39.3 us
    all_gather x1, waiting for transfers between devices, local(): lax.all_gather(normalized.astype(jnp.bfloat16), 'fsdp', axis=1, tiled=True)  29.1 us
    all_to_all x1, blocking collectives, local(): lax.all_to_all(split_up.astype(jnp.bfloat16), 'dp', split_axis=2, concat_...  18.8 us
    dot_general x3, matrix products, newton_schulz(): lax.dot_general(current, current, (((1,), (1,)), ((), ())), precision=lax...  10.2 us
    dot_general x3, matrix products, newton_schulz(): jnp.dot(combined, current, precision=lax.Precision.HIGHEST, preferred_ele...  9.1 us
  transfers between devices with their start and end apart: 6, of which 5 were waited for; matrix products, arithmetic and copies ran while one was open for 0% of the time, Pallas kernels for 0%

commit v1 on v0

--- a/solution.py
+++ b/solution.py
@@ -1,3 +1,4 @@
+import functools
 import math
 import jax
 import jax.numpy as jnp
@@ -18,6 +19,13 @@
 epsilon = 1e-07
 
 
+def array_recast(values, ax_name):
+    return jnp.sum(lax.all_gather(values, ax_name), 0)
+
+
+indices_produce = functools.partial(array_recast, ax_name="dp")
+
+
 def column_factors(global_peaks, clip_threshold):
     largest = jnp.max(global_peaks, axis=0).astype(jnp.float32)
     clip_ratio = jnp.minimum(1.0, clip_threshold.astype(jnp.float32)[0] / largest)
@@ -30,7 +38,7 @@
 
 
 def gram_over_replicas(partial_gram):
-    return lax.psum(partial_gram.astype(jnp.bfloat16), "dp").astype(jnp.float32)
+    return indices_produce(partial_gram.astype(jnp.bfloat16)).astype(jnp.float32)
 
 
 def newton_schulz(column_block, gram_sum):

time: 394 us -> 346 us (0.88)
  waiting for transfers between devices: 238 us -> 184 us
  other arithmetic: 9.38 us -> 18.5 us
  matrix products: 25 us -> 20.6 us
    psum x3 -> x0, waiting for transfers between devices: 161 us -> none  [gram_over_replicas(): return lax.psum(partial_gram.astype(jnp.bfloat16), 'dp').astype(jnp.float32)]
    all_gather x0 -> x3, waiting for transfers between devices: none -> 107 us  [array_recast(): return jnp.sum(lax.all_gather(values, ax_name), 0)]
    reduce_sum x0 -> x3, other arithmetic: none -> 9.17 us  [array_recast(): return jnp.sum(lax.all_gather(values, ax_name), 0)]
    dot_general x3, matrix products: 5.7 us -> 1.3 us  [newton_schulz(): jnp.dot(square, square, precision=lax.Precision.HIGHEST, preferred_elemen...]
where the time goes in v1:
time: 346 us
  waiting for transfers between devices  184 us (53%)
  blocking collectives  97.6 us (28%)
  matrix products  20.6 us (6%)
  other arithmetic  18.5 us (5%)
  between operations  17.5 us (5%)
  local copies, waits for them, and re-layouts  6.77 us (2%)
    all_gather x3, waiting for transfers between devices, array_recast(): return jnp.sum(lax.all_gather(values, ax_name), 0)  107 us
    reduce_scatter x1, waiting for transfers between devices, local(): lax.psum_scatter(replica_shard.astype(jnp.bfloat16), 'dp', scatter_dimens...  47.2 us
    psum x1, blocking collectives, local(): square_total = lax.psum(jnp.sum(blended * blended), ('dp', 'fsdp'))  39.5 us
    pmax x1, blocking collectives, local(): global_peaks = lax.pmax(logit_peaks, ('dp', 'fsdp'))  39.4 us
    all_gather x1, waiting for transfers between devices, local(): lax.all_gather(normalized.astype(jnp.bfloat16), 'fsdp', axis=1, tiled=True)  29.1 us
    all_to_all x1, blocking collectives, local(): lax.all_to_all(split_up.astype(jnp.bfloat16), 'dp', split_axis=2, concat_...  18.8 us
    dot_general x3, matrix products, newton_schulz(): lax.dot_general(current, current, (((1,), (1,)), ((), ())), precision=lax...  10.2 us
    reduce_sum x3, other arithmetic, array_recast(): return jnp.sum(lax.all_gather(values, ax_name), 0)  9.17 us
  transfers between devices with their start and end apart: 6, of which 5 were waited for; matrix products, arithmetic and copies ran while one was open for 0% of the time, Pallas kernels for 0%

profile of v1, /device:TPU:0, one launch (start us, length us, event | category | flops | bytes accessed | tf_op | source)
XLA Modules:
  0.0 345.9 jit_solution(12184027605742117671)
XLA Ops:
  7.2 0.7 reduce-scatter.2.cloned.1.call-update
  8.0 47.2 %reduce-scatter.2.cloned.1.call-done = bf16[64,2048]{1,0:T(8,128)(2,1)} async-done(((bf16[512,2048]{1,0:T(8,128)(2,1)}), bf16[64,2048]{1,0:T(8,128)(2,1)}) %reduce-scatter.2.cloned.1.call-update) | async-done | bytes 262160 | tf_op jit(solution)/shard_map/reduce_scatter | solution.py:66
  55.1 1.7 multiply_reduce_fusion
  56.8 39.5 %psum.7 = f32[]{:T(128)} all-reduce(f32[]{:T(128)} %get-tuple-element.3), channel_id=1, replica_groups=mesh['dp'=8,'fsdp'=4] {'dp','fsdp'}, use_global_device_ids=true, to_apply=%region_2.0 | all-reduce | flops 1 | bytes 8 | tf_op jit(solution)/shard_map/psum | solution.py:72
  97.0 1.7 divide_convert_fusion
  98.8 29.1 %all-gather.10.cloned.1.call-done = bf16[64,8192]{1,0:T(8,128)(2,1)} async-done(((bf16[64,2048]{1,0:T(8,128)(2,1)}), bf16[64,8192]{1,0:T(8,128)(2,1)}) %all-gather.10.cloned.1.call-update) | async-done | bytes 1048592 | tf_op jit(solution)/shard_map/all_gather | solution.py:80
  127.9 1.5 copy.11
  129.3 0.4 copy.8
  129.8 18.8 %all_to_all.18 = bf16[64,4,8,256]{3,1,0,2:T(4,128)(2,1)S(1)} all-to-all(bf16[64,4,8,256]{3,1,0,2:T(4,128)(2,1)S(1)} %copy.8), channel_id=1, replica_groups=mesh['dp'=8,'fsdp'=4] {'dp'}, dimensions={2} | all-to-all | bytes 2097152 | tf_op jit(solution)/shard_map/all_to_all | solution.py:84
  148.8 1.5 convolution_convert_fusion.2
  150.4 34.2 %all-gather.12.cloned.1.call-done = bf16[4096,512]{1,0:T(8,128)(2,1)} async-done(((bf16[512,512]{1,0:T(8,128)(2,1)}), bf16[4096,512]{1,0:T(8,128)(2,1)}) %all-gather.12.cloned.1.call-update) | async-done | bytes 4194320 | tf_op jit(solution)/shard_map/all_gather | solution.py:23
  184.6 3.1 reduce_sum.46
  187.7 0.4 fusion.5
  188.1 1.8 multiply_add_fusion.2
  190.0 1.3 copy-done
  191.3 4.3 %convolution_convert_fusion.1 = bf16[512,512]{1,0:T(8,128)(2,1)} fusion(f32[512,1024]{1,0:T(8,128)S(1)} %multiply_add_fusion.2), kind=kOutput, calls=%fused_computation.14 | convolution fusion | flops 3221487616 | bytes 2621440 | tf_op jit(solution)/shard_map/dot_general | solution.py:47
  195.9 36.5 %all-gather.14.cloned.1.call-done = bf16[4096,512]{1,0:T(8,128)(2,1)} async-done(((bf16[512,512]{1,0:T(8,128)(2,1)}), bf16[4096,512]{1,0:T(8,128)(2,1)}) %all-gather.14.cloned.1.call-update) | async-done | bytes 4194320 | tf_op jit(solution)/shard_map/all_gather | solution.py:23
  232.4 3.1 reduce_sum.47
  235.5 0.4 fusion.4
  235.9 1.1 copy-done.1
  237.1 3.7 %multiply_add_fusion.1 = f32[512,1024]{1,0:T(8,128)S(1)} fusion(f32[512,1024]{1,0:T(8,128)S(1)} %copy-done.1, f32[512,512]{1,0:T(8,128)S(1)} %fusion.4), kind=kOutput, calls=%fused_computation.5 | convolution fusion | flops 3222274048 | bytes 5242880 | tf_op jit(solution)/shard_map/dot_general | solution.py:58
  240.7 4.3 %convolution_convert_fusion = bf16[512,512]{1,0:T(8,128)(2,1)} fusion(f32[512,1024]{1,0:T(8,128)S(1)} %multiply_add_fusion.1), kind=kOutput, calls=%fused_computation.13 | convolution fusion | flops 3221487616 | bytes 2621440 | tf_op jit(solution)/shard_map/dot_general | solution.py:47
  245.1 0.3 all-gather.18.cloned.1.call-start
  245.4 36.5 %all-gather.16.cloned.1.call-done = bf16[4096,512]{1,0:T(8,128)(2,1)} async-done(((bf16[512,512]{1,0:T(8,128)(2,1)}), bf16[4096,512]{1,0:T(8,128)(2,1)}) %all-gather.16.cloned.1.call-update) | async-done | bytes 4194320 | tf_op jit(solution)/shard_map/all_gather | solution.py:23
  281.8 3.1 reduce_sum.48
  284.9 0.4 fusion.3
  285.3 3.6 %multiply_add_fusion = bf16[512,1024]{1,0:T(8,128)(2,1)S(1)} fusion(f32[512,1024]{1,0:T(8,128)S(1)} %multiply_add_fusion.1, f32[512,512]{1,0:T(8,128)S(1)} %fusion.3), kind=kOutput, calls=%fused_computation.4 | convolution fusion | flops 3222798336 | bytes 4194304 | tf_op jit(solution)/shard_map/dot_general | solution.py:58
  288.9 0.8 reshape.40
  289.7 0.5 constant_dynamic-slice_fusion
  290.3 0.7 copy.15
  291.1 39.4 %pmax.7 = s32[1,32]{1,0:T(1,128)S(1)} all-reduce(s32[1,32]{1,0:T(1,128)S(1)} %copy-done.4), channel_id=1, replica_groups=mesh['dp'=8,'fsdp'=4] {'dp','fsdp'}, use_global_device_ids=true, to_apply=%region_6.0 | all-reduce | flops 32 | bytes 256 | tf_op jit(solution)/shard_map/pmax | solution.py:71
  332.0 5.9 %fusion.2 = f32[512,2048]{1,0:T(8,128)} fusion(f32[512,2048]{1,0:T(8,128)} %param.7, bf16[512,1,2048]{2,0,1:T(8,128)(2,1)} %all-gather.18.cloned.1.call-done, f32[2048]{0:T(1024)S(1)} %dynamic_slice.8), kind=kLoop, calls=%fused_computation.3 | loop fusion | flops 7340032 | bytes 10493952 | tf_op jit(solution)/shard_map/mul | solution.py:100
  (25 shorter events, 0.8 us)
Async XLA Ops:
  7.2 48.0 %copy-start.3 = (f32[64,2048]{1,0:T(8,128)S(1)}, f32[64,2048]{1,0:T(8,128)}, u32[]{:S(2)}) copy-start(f32[64,2048]{1,0:T(8,128)} %param.6) | copy-start | bytes 1572868
  7.2 48.0 %reduce-scatter.2.cloned.1.call-start = ((), (), s32[]{:S(2)}) async-start(), calls=%async_computation.2 | async-start | bytes 2359296 | tf_op jit(solution)/shard_map/reduce_scatter | solution.py:66
  7.9 119.9 %all-gather.10.cloned.1.call-start = ((), (), s32[]{:S(2)}) async-start(), calls=%async_computation.3 | async-start | bytes 1310720 | tf_op jit(solution)/shard_map/all_gather | solution.py:80
  56.8 72.9 %copy-start.2 = (f32[64,2048]{1,0:T(8,128)}, f32[64,2048]{1,0:T(8,128)S(1)}, u32[]{:S(2)}) copy-start(f32[64,2048]{1,0:T(8,128)S(1)} %get-tuple-element.4) | copy-start | bytes 1572868
  98.7 85.9 %all-gather.12.cloned.1.call-start = ((), (), s32[]{:S(2)}) async-start(), calls=%async_computation.4 | async-start | bytes 4718592 | tf_op jit(solution)/shard_map/all_gather | solution.py:23
  150.3 82.1 %all-gather.14.cloned.1.call-start = ((), (), s32[]{:S(2)}) async-start(), calls=%async_computation.5 | async-start | bytes 4718592 | tf_op jit(solution)/shard_map/all_gather | solution.py:23
  190.0 1.3 copy-start
  195.7 86.1 %all-gather.16.cloned.1.call-start = ((), (), s32[]{:S(2)}) async-start(), calls=%async_computation.6 | async-start | bytes 4718592 | tf_op jit(solution)/shard_map/all_gather | solution.py:23
  235.5 1.6 copy-start.1
  245.1 86.9 %all-gather.18.cloned.1.call-start = ((), (), s32[]{:S(2)}) async-start(), calls=%async_computation.7 | async-start | bytes 2359296 | tf_op jit(solution)/shard_map/all_gather | solution.py:91
  288.9 2.1 copy-start.4
Sparse Core Ops, SparseCore 0:
  11.3 43.8 reduce-scatter.1
  98.9 28.9 all-gather.9
  150.5 34.1 all-gather.11
  195.8 36.5 all-gather.13
  245.2 36.5 all-gather.15
  291.2 28.1 all-gather.17
